TPU v7x, 256 devices: a whole 4x4x8 slice. The times are simulated.
256 devices in a mesh: dom: 64 (over y, z, core), rep: 4 (over x).
Axes of the slice: x: 4, y: 4, z: 8, core: 2. Of those that a mesh axis runs over, the one named last changes fastest.
Arguments:
- feats: bfloat16 [256, 262144], P('rep', 'dom'), may hold values from -6 to 6
- w_self: bfloat16 [256, 256], P(None, 'rep'), may hold values from -0.375 to 0.375
- w_neigh: bfloat16 [256, 256], P(None, 'rep'), may hold values from -3 to 3
- local_cols: int32 [2048, 2], P('dom'), may hold values from 0 to 31
- local_tiles: bfloat16 [2048, 2, 128, 128], P('dom'), may hold values from 0 to 3, as said below
- send_list: int32 [64, 64, 2], P('dom'), may hold values from 0 to 31
- remote_rows: int32 [64, 64, 2], P('dom'), may hold values from 0 to 31
- remote_tiles: bfloat16 [64, 64, 2, 128, 128], P('dom'), may hold values from 0 to 3, as said below
- cotangent: bfloat16 [256, 262144], P('rep', 'dom'), may hold values from -6 to 6
Outputs:
- output: bfloat16 [256, 262144], P('rep', 'dom')
- grad_feats: bfloat16 [256, 262144], P('rep', 'dom')
- grad_w_self: float32 [256, 256], P(None, 'rep')
- grad_w_neigh: float32 [256, 256], P(None, 'rep')
Inputs may be any that keep to these rules, and one draw needn't show every extreme that they name: `local_tiles`: edge weights: zero where a tile has no edge, positive otherwise. `remote_tiles`: edge weights: zero where a tile has no edge, positive otherwise.
All inputs are finite; a program needn't handle non-finite values.
Results may differ from a plain program's by a relative error of at most 0.0055.
Values may be sent and summed in bfloat16 or wider, within the bound.
No kernel may reach another device: no remote copies, remote signals or barrier semaphores. Data moves between devices by JAX's collectives and lax.ppermute only.
A program may use at most 128 MiB of HBM per device.

v0:
```python
import jax
import jax.numpy as jnp
from jax import lax
from jax.sharding import PartitionSpec as P


def local(
    feats, w_self, w_neigh, local_cols, local_tiles, send_list, remote_rows, remote_tiles, cotangent
):
    highest = lax.Precision.HIGHEST
    feat_width, node_count = feats.shape
    blocks, local_links, tile_side, _ = local_tiles.shape
    block_ids = jnp.arange(blocks, dtype=jnp.int32)
    blocked = feats.reshape(feat_width, blocks, tile_side)
    outgoing = blocked[:, send_list[0]]
    incoming = lax.all_to_all(outgoing, "dom", split_axis=1, concat_axis=1, tiled=True)
    full_feats = lax.all_gather(feats, "rep", axis=0, tiled=True)
    gathered = blocked[:, local_cols]
    summed = jnp.einsum("fblj,blij->fbi", gathered, local_tiles, preferred_element_type=jnp.float32)
    weight_rows = jnp.sum(local_tiles, axis=(1, 3), dtype=jnp.float32)
    far_tiles = remote_tiles[0]
    far_rows = remote_rows[0]
    placing = (far_rows[:, :, None] == block_ids).astype(jnp.float32)
    far_sums = jnp.sum(far_tiles, axis=3, dtype=jnp.float32)
    divisor = 1.0 + weight_rows + jnp.einsum("ski,skb->bi", far_sums, placing, precision=highest)
    far_terms = jnp.einsum(
        "fskj,skij->fski", incoming, far_tiles, preferred_element_type=jnp.float32
    )
    summed = summed + jnp.einsum("fski,skb->fbi", far_terms, placing, precision=highest)
    aggregate = (summed / divisor).astype(jnp.bfloat16).reshape(feat_width, node_count)
    full_agg = lax.all_gather(aggregate, "rep", axis=0, tiled=True)
    preact = jnp.einsum("ab,an->bn", w_self, full_feats, preferred_element_type=jnp.float32)
    preact = preact + jnp.einsum("ab,an->bn", w_neigh, full_agg, preferred_element_type=jnp.float32)
    sigmoid_val = jax.nn.sigmoid(preact)
    output = (preact * sigmoid_val).astype(jnp.bfloat16)
    slope = sigmoid_val * (1.0 + preact * (1.0 - sigmoid_val))
    grad_pre = (cotangent.astype(jnp.float32) * slope).astype(jnp.bfloat16)
    wg_self = jnp.einsum("an,bn->ab", full_feats, grad_pre, preferred_element_type=jnp.float32)
    wg_neigh = jnp.einsum("an,bn->ab", full_agg, grad_pre, preferred_element_type=jnp.float32)
    wg_self, wg_neigh = lax.psum((wg_self, wg_neigh), "dom")
    term_self = jnp.dot(w_self, grad_pre, preferred_element_type=jnp.float32)
    term_neigh = jnp.dot(w_neigh, grad_pre, preferred_element_type=jnp.float32)
    stacked = lax.psum_scatter(
        jnp.concatenate([term_self, term_neigh], axis=1), "rep", scatter_dimension=0, tiled=True
    )
    back_self = stacked[:, :node_count]
    back_agg = stacked[:, node_count:]
    scaled = (back_agg.reshape(feat_width, blocks, tile_side) / divisor).astype(jnp.bfloat16)
    picked = scaled[:, far_rows]
    far_back = jnp.einsum("fski,skij->fskj", picked, far_tiles, preferred_element_type=jnp.float32)
    returned = lax.all_to_all(far_back, "dom", split_axis=1, concat_axis=1, tiled=True)
    near_back = jnp.einsum(
        "fbi,blij->fblj", scaled, local_tiles, preferred_element_type=jnp.float32
    )
    landing = (local_cols[:, :, None] == block_ids).astype(jnp.float32)
    collected = jnp.einsum("fblj,blc->fcj", near_back, landing, precision=highest)
    homing = (send_list[0][:, :, None] == block_ids).astype(jnp.float32)
    collected = collected + jnp.einsum("fdkj,dkc->fcj", returned, homing, precision=highest)
    grad_feats = (back_self + collected.reshape(feat_width, node_count)).astype(jnp.bfloat16)
    return (output, grad_feats, wg_self, wg_neigh)


def solution(mesh):
    placed = (
        P("rep", "dom"),
        P(None, "rep"),
        P(None, "rep"),
        P("dom", None),
        P("dom", None, None, None),
        P("dom", None, None),
        P("dom", None, None),
        P("dom", None, None, None, None),
        P("rep", "dom"),
    )
    return jax.shard_map(
        local,
        mesh=mesh,
        in_specs=placed,
        out_specs=(P("rep", "dom"), P("rep", "dom"), P(None, "rep"), P(None, "rep")),
        check_vma=False,
    )
```

profile of v0, /device:TPU:1, one launch (start us, length us, event | category | flops | bytes accessed | tf_op | source)
XLA Modules:
  0.0 480.7 jit_solution(3183939513342969295)
XLA Ops:
  9.3 2.1 gather_fusion.1
  11.5 13.3 %all-to-all-start = ((bf16[64,64,2,128]{3,0,2,1:T(8,128)(2,1)}), bf16[64,64,2,128]{3,0,2,1:T(8,128)(2,1)S(1)}, u32[]{:S(2)}, u32[]{:S(2)}) async-start(bf16[64,64,2,128]{3,0,2,1:T(8,128)(2,1)} %bitcast.123), calls=%async_computation | async-start | bytes 4194304 | tf_op jit(solution)/shard_map/all_to_all | solution.py:16
  25.0 1.7 gather_fusion
  26.7 2.2 convert_reduce_fusion.1
  28.9 3.4 convert_reduce_fusion
  32.5 43.5 %all-to-all-done = bf16[64,64,2,128]{3,0,2,1:T(8,128)(2,1)S(1)} async-done(((bf16[64,64,2,128]{3,0,2,1:T(8,128)(2,1)}), bf16[64,64,2,128]{3,0,2,1:T(8,128)(2,1)S(1)}, u32[]{:S(2)}, u32[]{:S(2)}) %all-to-all-start) | async-done | bytes 2097184 | tf_op jit(solution)/shard_map/all_to_all | solution.py:16
  76.0 5.1 %fusion.8 = f32[64,64,2,128]{3,0,2,1:T(8,128)S(1)} fusion(bf16[64,64,2,128]{3,0,2,1:T(8,128)(2,1)S(1)} %all-to-all-done, bf16[1,64,2,128,128]{4,3,2,1,0:T(8,128)(2,1)} %param.16), kind=kOutput, calls=%fused_computation.18 | convolution fusion | flops 268435456 | bytes 10485760 | tf_op jit(solution)/shard_map/fskj,skij->fski/dot_general | solution.py:26
  81.2 4.0 fusion.20
  88.2 29.0 %all-gather.5.cloned.1.call-done = bf16[256,4096]{1,0:T(8,128)(2,1)} async-done(((bf16[64,4096]{1,0:T(8,128)(2,1)}), bf16[256,4096]{1,0:T(8,128)(2,1)}) %all-gather.5.cloned.1.call-update) | async-done | bytes 2097168 | tf_op jit(solution)/shard_map/all_gather | solution.py:31
  117.2 2.1 convolution_bitcast_fusion.2
  119.2 33.2 %all-gather.3.cloned.1.call-done = bf16[256,4096]{1,0:T(8,128)(2,1)} async-done(((bf16[64,4096]{1,0:T(8,128)(2,1)}), bf16[256,4096]{1,0:T(8,128)(2,1)}) %all-gather.3.cloned.1.call-update) | async-done | bytes 2097168 | tf_op jit(solution)/shard_map/all_gather | solution.py:17
  152.4 3.2 multiply_convert_fusion
  157.1 3.8 pad_maximum_fusion
  160.9 8.9 %copy.60 = f32[256,8192]{1,0:T(8,128)} copy(f32[256,8192]{0,1:T(8,128)} %pad_maximum_fusion) | data formatting | bytes 16777216
  170.1 83.0 %reduce-scatter.4.cloned.1.call-done = f32[64,8192]{1,0:T(8,128)} async-done(((f32[256,8192]{1,0:T(8,128)}), f32[64,8192]{1,0:T(8,128)}) %reduce-scatter.4.cloned.1.call-update) | async-done | bytes 2097168
  253.1 3.1 fusion.49
  256.2 1.8 copy.63
  258.0 1.6 copy.48
  259.6 1.4 divide_convert_fusion
  261.9 5.4 %fusion.11 = f32[64,64,2,128]{3,0,2,1:T(8,128)} fusion(bf16[64,64,2,128]{3,0,2,1:T(8,128)(2,1)S(1)} %bitcast.121, bf16[1,64,2,128,128]{4,3,2,1,0:T(8,128)(2,1)} %param.16), kind=kOutput, calls=%fused_computation.19 | convolution fusion | flops 268435456 | bytes 10485760 | tf_op jit(solution)/shard_map/fski,skij->fskj/dot_general | solution.py:50
  267.3 11.0 %all-to-all-start.1 = ((f32[64,64,2,128]{3,0,2,1:T(8,128)}), f32[64,64,2,128]{3,0,2,1:T(8,128)}, u32[]{:S(2)}, u32[]{:S(2)}) async-start(f32[64,64,2,128]{3,0,2,1:T(8,128)} %fusion.11), calls=%async_computation.1 | async-start | bytes 8388608 | tf_op jit(solution)/shard_map/all_to_all | solution.py:51
  278.6 1.4 fusion.50
  280.2 1.4 convolution_bitcast_fusion.5
  281.6 3.4 copy.62
  285.4 2.1 fusion.17
  287.5 87.6 %all-to-all-done.1 = f32[64,64,2,128]{3,0,2,1:T(8,128)} async-done(((f32[64,64,2,128]{3,0,2,1:T(8,128)}), f32[64,64,2,128]{3,0,2,1:T(8,128)}, u32[]{:S(2)}, u32[]{:S(2)}) %all-to-all-start.1) | async-done | bytes 4194336 | tf_op jit(solution)/shard_map/all_to_all | solution.py:51
  375.1 5.9 %fusion.31 = f32[64,32,128]{2,1,0:T(8,128)S(1)} fusion(f32[32,64,128]{2,0,1:T(8,128)S(1)} %fusion.17, f32[64,64,2,128]{3,0,2,1:T(8,128)} %all-to-all-done.1, s32[64,2]{0,1:T(2,128)S(1)} %bitcast.128), kind=kOutput, calls=%fused_computation.32 | convolution fusion | flops 402919424 | bytes 6291968 | tf_op jit(solution)/shard_map/fdkj,dkc->fcj/dot_general | solution.py:58
  381.0 2.0 copy.59
  383.0 1.8 fusion.14
  386.0 85.2 %all-reduce.3.cloned.1.call-done = (f32[256,64]{0,1:T(8,128)}, f32[256,64]{0,1:T(8,128)}) async-done(((f32[256,64]{0,1:T(8,128)}, f32[256,64]{0,1:T(8,128)}), (f32[256,64]{0,1:T(8,128)}, f32[256,64]{0,1:T(8,128)})) %all-reduce.3.cloned.1.call-update) | async-done | bytes 131088 | tf_op jit(solution)/shard_map/psum | solution.py:40
  471.2 1.5 copy.90
  472.7 1.5 copy.91
  (55 shorter events, 10.3 us)
Async XLA Ops:
  7.2 145.3 %copy-start = (bf16[256,64]{0,1:T(8,128)(2,1)S(1)}, bf16[256,64]{0,1:T(8,128)(2,1)}, u32[]{:S(2)}) copy-start(bf16[256,64]{0,1:T(8,128)(2,1)} %param.10) | copy-start | bytes 98308
  11.5 13.3 %copy-start.10 = (s32[32,2]{0,1:T(2,128)S(1)}, s32[32,2]{0,1:T(2,128)}, u32[]{:S(2)}) copy-start(s32[32,2]{0,1:T(2,128)} %param.12) | copy-start | bytes 772
  11.5 64.5 %all-to-all-start = ((bf16[64,64,2,128]{3,0,2,1:T(8,128)(2,1)}), bf16[64,64,2,128]{3,0,2,1:T(8,128)(2,1)S(1)}, u32[]{:S(2)}, u32[]{:S(2)}) async-start(bf16[64,64,2,128]{3,0,2,1:T(8,128)(2,1)} %bitcast.123), calls=%async_computation | async-start | bytes 4194304 | tf_op jit(solution)/shard_map/all_to_all | solution.py:16
  24.8 92.4 %all-gather.5.cloned.1.call-start = ((), (), s32[]{:S(2)}) async-start(), calls=%async_computation.4 | async-start | bytes 2621440 | tf_op jit(solution)/shard_map/all_gather | solution.py:31
  28.9 3.4 copy-start.9
  81.1 4.0 copy-start.2
  81.1 4.0 copy-start.7
  86.3 30.9 %copy-start.8 = (bf16[256,64]{0,1:T(8,128)(2,1)S(1)}, bf16[256,64]{0,1:T(8,128)(2,1)}, u32[]{:S(2)}) copy-start(bf16[256,64]{0,1:T(8,128)(2,1)} %param.11) | copy-start | bytes 98308
  87.2 65.3 %copy-start.12 = (bf16[64,4096]{1,0:T(8,128)(2,1)S(1)}, bf16[64,4096]{1,0:T(8,128)(2,1)}, u32[]{:S(2)}) copy-start(bf16[64,4096]{1,0:T(8,128)(2,1)} %param.17) | copy-start | bytes 1572868
  87.2 65.3 %all-gather.3.cloned.1.call-start = ((), (), s32[]{:S(2)}) async-start(), calls=%async_computation.3 | async-start | bytes 2621440 | tf_op jit(solution)/shard_map/all_gather | solution.py:17
  87.9 165.2 %reduce-scatter.4.cloned.1.call-start = ((), (), s32[]{:S(2)}) async-start(), calls=%async_computation.5 | async-start | bytes 10485760
  267.3 11.2 %copy-start.4 = (bf16[256,4096]{1,0:T(8,128)(2,1)S(1)}, bf16[256,4096]{1,0:T(8,128)(2,1)}, u32[]{:S(2)}) copy-start(bf16[256,4096]{1,0:T(8,128)(2,1)} %all-gather.5.cloned.1.call-done) | copy-start | bytes 6291460
  267.3 107.7 %all-to-all-start.1 = ((f32[64,64,2,128]{3,0,2,1:T(8,128)}), f32[64,64,2,128]{3,0,2,1:T(8,128)}, u32[]{:S(2)}, u32[]{:S(2)}) async-start(f32[64,64,2,128]{3,0,2,1:T(8,128)} %fusion.11), calls=%async_computation.1 | async-start | bytes 8388608 | tf_op jit(solution)/shard_map/all_to_all | solution.py:51
  278.3 192.9 %all-reduce.3.cloned.1.call-start = ((), (), s32[]{:S(2)}) async-start(), calls=%async_computation.6 | async-start | bytes 262144 | tf_op jit(solution)/shard_map/psum | solution.py:40
  278.6 1.6 copy-start.6
  281.6 3.4 copy-start.3
  285.4 89.6 %copy-start.11 = (s32[1,64,2]{1,2,0:T(2,128)S(1)}, s32[1,64,2]{1,2,0:T(2,128)}, u32[]{:S(2)}) copy-start(s32[1,64,2]{1,2,0:T(2,128)} %param.14) | copy-start | bytes 1540
  381.0 2.0 copy-start.5
  383.0 91.1 %copy-start.1 = (bf16[256,64]{0,1:T(8,128)(2,1)S(1)}, bf16[256,64]{0,1:T(8,128)(2,1)}, u32[]{:S(2)}) copy-start(bf16[256,64]{0,1:T(8,128)(2,1)} %param.10) | copy-start | bytes 98308
Sparse Core Ops, SparseCore 0:
  87.3 29.8 all-gather.4
  119.0 33.4 all-gather.2
  169.9 83.1 reduce-scatter.3
  283.0 188.1 all-reduce.2
where the time goes:
time: 482 us; the launch traced here: 481 us
  waiting for transfers between devices  362 us (75%)
  matrix products  33.7 us (7%)
  local copies, waits for them, and re-layouts  32.6 us (7%)
  starting transfers between devices  24.8 us (5%)
  between operations  14 us (3%)
  other arithmetic  13.2 us (3%)
    all_to_all x1, waiting for transfers between devices, local(): lax.all_to_all(far_back, 'dom', split_axis=1, concat_axis=1, tiled=True)  87.6 us
    psum x1, waiting for transfers between devices, local(): wg_self, wg_neigh = lax.psum((wg_self, wg_neigh), 'dom')  85.2 us
    unnamed x5, waiting for transfers between devices  83.8 us
    all_to_all x1, waiting for transfers between devices, local(): lax.all_to_all(outgoing, 'dom', split_axis=1, concat_axis=1, tiled=True)  43.5 us
    all_gather x1, waiting for transfers between devices, local(): full_feats = lax.all_gather(feats, 'rep', axis=0, tiled=True)  33.2 us
    all_gather x1, waiting for transfers between devices, local(): full_agg = lax.all_gather(aggregate, 'rep', axis=0, tiled=True)  29 us
    unnamed x32, local copies, waits for them, and re-layouts  18.5 us
    all_to_all x1, starting transfers between devices, local(): lax.all_to_all(outgoing, 'dom', split_axis=1, concat_axis=1, tiled=True)  13.3 us
  transfers between devices with their start and end apart: 6, of which 6 were waited for; matrix products, arithmetic and copies ran while one was open for 6% of the time, Pallas kernels for 0%

commit v1 on v0

--- a/solution.py
+++ b/solution.py
@@ -14,7 +14,12 @@
     blocked = feats.reshape(feat_width, blocks, tile_side)
     outgoing = blocked[:, send_list[0]]
     incoming = lax.all_to_all(outgoing, "dom", split_axis=1, concat_axis=1, tiled=True)
-    full_feats = lax.all_gather(feats, "rep", axis=0, tiled=True)
+    ring = [feats]
+    for hop in range(3):
+        ring.append(lax.ppermute(ring[-1], "rep", [(dev, (dev + 1) % 4) for dev in range(4)]))
+    full_feats = jnp.roll(
+        jnp.concatenate(ring[::-1], axis=0), (lax.axis_index("rep") + 1) * ring[0].shape[0], axis=0
+    )
     gathered = blocked[:, local_cols]
     summed = jnp.einsum("fblj,blij->fbi", gathered, local_tiles, preferred_element_type=jnp.float32)
     weight_rows = jnp.sum(local_tiles, axis=(1, 3), dtype=jnp.float32)

time: 482 us -> 451 us (0.936)
  waiting for transfers between devices: 362 us -> 314 us
  local copies, waits for them, and re-layouts: 32.6 us -> 43.1 us
    all_to_all x1, waiting for transfers between devices: 43.5 us -> 9.63 us  [local(): lax.all_to_all(outgoing, 'dom', split_axis=1, concat_axis=1, tiled=True)]
    all_gather x1 -> x0, waiting for transfers between devices: 33.2 us -> none  [local(): full_feats = lax.all_gather(feats, 'rep', axis=0, tiled=True)]
    ppermute x0 -> x3, waiting for transfers between devices: none -> 31.7 us  [local(): lax.ppermute(ring[-1], 'rep', [(dev, (dev + 1) % 4) for dev in range(4)])]
    unnamed x32 -> x37, local copies, waits for them, and re-layouts: 18.5 us -> 28.1 us
    all_gather x1, waiting for transfers between devices: 29 us -> 19.7 us  [local(): full_agg = lax.all_gather(aggregate, 'rep', axis=0, tiled=True)]
    unnamed x5 -> x4, waiting for transfers between devices: 83.8 us -> 83.4 us
  transfers between devices with their start and end apart: 6 -> 8, of which waited for: 6 -> 8; matrix products, arithmetic and copies ran while one was open for 6% -> 9% of each run, Pallas kernels for 0% -> 0%
where the time goes in v1:
time: 451 us; the launch traced here: 450 us
  waiting for transfers between devices  314 us (70%)
  local copies, waits for them, and re-layouts  43.1 us (10%)
  matrix products  38.5 us (9%)
  starting transfers between devices  25.9 us (6%)
  between operations  14 us (3%)
  other arithmetic  13.9 us (3%)
    psum x1, waiting for transfers between devices, local(): wg_self, wg_neigh = lax.psum((wg_self, wg_neigh), 'dom')  86.6 us
    all_to_all x1, waiting for transfers between devices, local(): lax.all_to_all(far_back, 'dom', split_axis=1, concat_axis=1, tiled=True)  83.5 us
    unnamed x4, waiting for transfers between devices  83.4 us
    ppermute x3, waiting for transfers between devices, local(): lax.ppermute(ring[-1], 'rep', [(dev, (dev + 1) % 4) for dev in range(4)])  31.7 us
    unnamed x37, local copies, waits for them, and re-layouts  28.1 us
    all_gather x1, waiting for transfers between devices, local(): full_agg = lax.all_gather(aggregate, 'rep', axis=0, tiled=True)  19.7 us
    all_to_all x1, starting transfers between devices, local(): lax.all_to_all(outgoing, 'dom', split_axis=1, concat_axis=1, tiled=True)  13.2 us
    all_to_all x1, starting transfers between devices, local(): lax.all_to_all(far_back, 'dom', split_axis=1, concat_axis=1, tiled=True)  10.8 us
  transfers between devices with their start and end apart: 8, of which 8 were waited for; matrix products, arithmetic and copies ran while one was open for 9% of the time, Pallas kernels for 0%

profile of v1, /device:TPU:1, one launch (start us, length us, event | category | flops | bytes accessed | tf_op | source)
XLA Modules:
  0.0 449.9 jit_solution(12283403160150713281)
XLA Ops:
  10.3 2.1 gather_fusion.1
  12.4 13.2 %all-to-all-start = ((bf16[64,64,2,128]{3,0,2,1:T(8,128)(2,1)}), bf16[64,64,2,128]{3,0,2,1:T(8,128)(2,1)S(1)}, u32[]{:S(2)}, u32[]{:S(2)}) async-start(bf16[64,64,2,128]{3,0,2,1:T(8,128)(2,1)} %bitcast.119), calls=%async_computation | async-start | bytes 4194304 | tf_op jit(solution)/shard_map/all_to_all | solution.py:16
  26.9 13.1 %collective-permute-done = bf16[64,4096]{1,0:T(8,128)(2,1)} collective-permute-done((bf16[64,4096]{1,0:T(8,128)(2,1)S(1)}, bf16[64,4096]{1,0:T(8,128)(2,1)}, u32[]{:S(2)}, u32[]{:S(2)}) %collective-permute-start) | collective-permute-done | bytes 524320 | tf_op jit(solution)/shard_map/ppermute | solution.py:19
  42.0 2.2 convert_reduce_fusion.1
  44.2 9.5 %collective-permute-done.1 = bf16[64,4096]{1,0:T(8,128)(2,1)} collective-permute-done((bf16[64,4096]{1,0:T(8,128)(2,1)}, bf16[64,4096]{1,0:T(8,128)(2,1)}, u32[]{:S(2)}, u32[]{:S(2)}) %collective-permute-start.1) | collective-permute-done | bytes 524320 | tf_op jit(solution)/shard_map/ppermute | solution.py:19
  53.7 3.4 convert_reduce_fusion
  57.3 9.0 %collective-permute-done.2 = bf16[64,4096]{1,0:T(8,128)(2,1)S(1)} collective-permute-done((bf16[64,4096]{1,0:T(8,128)(2,1)}, bf16[64,4096]{1,0:T(8,128)(2,1)S(1)}, u32[]{:S(2)}, u32[]{:S(2)}) %collective-permute-start.2) | collective-permute-done | bytes 524320 | tf_op jit(solution)/shard_map/ppermute | solution.py:19
  67.2 9.6 %all-to-all-done = bf16[64,64,2,128]{3,0,2,1:T(8,128)(2,1)S(1)} async-done(((bf16[64,64,2,128]{3,0,2,1:T(8,128)(2,1)}), bf16[64,64,2,128]{3,0,2,1:T(8,128)(2,1)S(1)}, u32[]{:S(2)}, u32[]{:S(2)}) %all-to-all-start) | async-done | bytes 2097184 | tf_op jit(solution)/shard_map/all_to_all | solution.py:16
  76.8 5.2 %fusion.9 = f32[64,64,2,128]{3,0,2,1:T(8,128)S(1)} fusion(bf16[64,64,2,128]{3,0,2,1:T(8,128)(2,1)S(1)} %all-to-all-done, bf16[1,64,2,128,128]{4,3,2,1,0:T(8,128)(2,1)} %param.16), kind=kOutput, calls=%fused_computation.18 | convolution fusion | flops 268435456 | bytes 10485760 | tf_op jit(solution)/shard_map/fskj,skij->fski/dot_general | solution.py:31
  82.0 4.0 fusion.24
  88.3 1.9 constant_dynamic-update-slice_fusion.6
  90.1 1.9 constant_dynamic-update-slice_fusion.5
  93.7 1.9 constant_dynamic-update-slice_fusion.2
  95.5 1.9 constant_dynamic-update-slice_fusion.1
  98.3 19.7 %all-gather.2.cloned.1.call-done = bf16[256,4096]{1,0:T(8,128)(2,1)} async-done(((bf16[64,4096]{1,0:T(8,128)(2,1)}), bf16[256,4096]{1,0:T(8,128)(2,1)}) %all-gather.2.cloned.1.call-update) | async-done | bytes 2097168 | tf_op jit(solution)/shard_map/all_gather | solution.py:36
  118.0 2.1 fusion.57
  120.1 3.2 multiply_convert_fusion
  124.8 3.8 pad_maximum_fusion
  128.5 8.9 %copy.60 = f32[256,8192]{1,0:T(8,128)} copy(f32[256,8192]{0,1:T(8,128)} %pad_maximum_fusion) | data formatting | bytes 16777216
  137.5 83.3 %reduce-scatter.4.cloned.1.call-done = f32[64,8192]{1,0:T(8,128)} async-done(((f32[256,8192]{1,0:T(8,128)}), f32[64,8192]{1,0:T(8,128)}) %reduce-scatter.4.cloned.1.call-update) | async-done | bytes 2097168
  220.8 3.1 fusion.55
  223.8 1.8 copy.63
  229.6 5.4 %fusion.12 = f32[64,64,2,128]{3,0,2,1:T(8,128)} fusion(bf16[64,64,2,128]{3,0,2,1:T(8,128)(2,1)S(1)} %bitcast.117, bf16[1,64,2,128,128]{4,3,2,1,0:T(8,128)(2,1)} %param.16), kind=kOutput, calls=%fused_computation.19 | convolution fusion | flops 268435456 | bytes 10485760 | tf_op jit(solution)/shard_map/fski,skij->fskj/dot_general | solution.py:55
  235.0 10.8 %all-to-all-start.1 = ((f32[64,64,2,128]{3,0,2,1:T(8,128)}), f32[64,64,2,128]{3,0,2,1:T(8,128)}, u32[]{:S(2)}, u32[]{:S(2)}) async-start(f32[64,64,2,128]{3,0,2,1:T(8,128)} %fusion.12), calls=%async_computation.1 | async-start | bytes 8388608 | tf_op jit(solution)/shard_map/all_to_all | solution.py:56
  246.2 3.2 fusion.18
  249.3 3.0 fusion.56
  252.3 3.2 copy.62
  256.0 3.0 fusion.21
  259.0 83.5 %all-to-all-done.1 = f32[64,64,2,128]{3,0,2,1:T(8,128)} async-done(((f32[64,64,2,128]{3,0,2,1:T(8,128)}), f32[64,64,2,128]{3,0,2,1:T(8,128)}, u32[]{:S(2)}, u32[]{:S(2)}) %all-to-all-start.1) | async-done | bytes 4194336 | tf_op jit(solution)/shard_map/all_to_all | solution.py:56
  342.5 6.4 %fusion.35 = f32[64,32,128]{2,1,0:T(8,128)S(1)} fusion(f32[32,64,128]{2,0,1:T(8,128)} %fusion.21, f32[64,64,2,128]{3,0,2,1:T(8,128)} %all-to-all-done.1, s32[64,2]{0,1:T(2,128)S(1)} %bitcast.124), kind=kOutput, calls=%fused_computation.35 | convolution fusion | flops 402919424 | bytes 6291968 | tf_op jit(solution)/shard_map/fdkj,dkc->fcj/dot_general | solution.py:63
  348.9 2.0 copy.59
  353.9 86.6 %all-reduce.3.cloned.1.call-done = (f32[256,64]{0,1:T(8,128)}, f32[256,64]{0,1:T(8,128)}) async-done(((f32[256,64]{0,1:T(8,128)}, f32[256,64]{0,1:T(8,128)}), (f32[256,64]{0,1:T(8,128)}, f32[256,64]{0,1:T(8,128)})) %all-reduce.3.cloned.1.call-update) | async-done | bytes 131088 | tf_op jit(solution)/shard_map/psum | solution.py:45
  (63 shorter events, 24.1 us)
Async XLA Ops:
  7.2 112.9 %copy-start = (bf16[256,64]{0,1:T(8,128)(2,1)S(1)}, bf16[256,64]{0,1:T(8,128)(2,1)}, u32[]{:S(2)}) copy-start(bf16[256,64]{0,1:T(8,128)(2,1)} %param.10) | copy-start | bytes 98308
  10.2 15.4 %copy-start.5 = (bf16[64,4096]{1,0:T(8,128)(2,1)S(1)}, bf16[64,4096]{1,0:T(8,128)(2,1)}, u32[]{:S(2)}) copy-start(bf16[64,4096]{1,0:T(8,128)(2,1)} %param.9) | copy-start | bytes 1572868
  10.2 29.8 %copy-start.9 = (s32[32,2]{0,1:T(2,128)S(1)}, s32[32,2]{0,1:T(2,128)}, u32[]{:S(2)}) copy-start(s32[32,2]{0,1:T(2,128)} %param.12) | copy-start | bytes 772
  12.4 64.4 %all-to-all-start = ((bf16[64,64,2,128]{3,0,2,1:T(8,128)(2,1)}), bf16[64,64,2,128]{3,0,2,1:T(8,128)(2,1)S(1)}, u32[]{:S(2)}, u32[]{:S(2)}) async-start(bf16[64,64,2,128]{3,0,2,1:T(8,128)(2,1)} %bitcast.119), calls=%async_computation | async-start | bytes 4194304 | tf_op jit(solution)/shard_map/all_to_all | solution.py:16
  25.6 92.4 %all-gather.2.cloned.1.call-start = ((), (), s32[]{:S(2)}) async-start(), calls=%async_computation.3 | async-start | bytes 2621440 | tf_op jit(solution)/shard_map/all_gather | solution.py:36
  25.6 14.4 %collective-permute-start = (bf16[64,4096]{1,0:T(8,128)(2,1)S(1)}, bf16[64,4096]{1,0:T(8,128)(2,1)}, u32[]{:S(2)}, u32[]{:S(2)}) collective-permute-start(bf16[64,4096]{1,0:T(8,128)(2,1)S(1)} %copy-done.5), channel_id=1, source_target_pairs={{0,1},{1,2},{2,3},{3,0},{4,5},{5,6},{6,7},{7,4},{8,9},{9,10},{10,1... | collective-permute-start | bytes 1572872 | tf_op jit(solution)/shard_map/ppermute | solution.py:19
  40.1 13.6 %collective-permute-start.1 = (bf16[64,4096]{1,0:T(8,128)(2,1)}, bf16[64,4096]{1,0:T(8,128)(2,1)}, u32[]{:S(2)}, u32[]{:S(2)}) collective-permute-start(bf16[64,4096]{1,0:T(8,128)(2,1)} %collective-permute-done), channel_id=1, source_target_pairs={{0,1},{1,2},{2,3},{3,0},{4,5},{5,6},{6,7},{7,4},{8,9},{9,10},{10,1... | collective-permute-start | bytes 1572872 | tf_op jit(solution)/shard_map/ppermute | solution.py:19
  40.3 16.8 %copy-start.8 = (s32[1,64,2]{1,2,0:T(2,128)S(1)}, s32[1,64,2]{1,2,0:T(2,128)}, u32[]{:S(2)}) copy-start(s32[1,64,2]{1,2,0:T(2,128)} %param.15) | copy-start | bytes 1540
  53.7 12.6 %collective-permute-start.2 = (bf16[64,4096]{1,0:T(8,128)(2,1)}, bf16[64,4096]{1,0:T(8,128)(2,1)S(1)}, u32[]{:S(2)}, u32[]{:S(2)}) collective-permute-start(bf16[64,4096]{1,0:T(8,128)(2,1)} %collective-permute-done.1), channel_id=1, source_target_pairs={{0,1},{1,2},{2,3},{3,0},{4,5},{5,6},{6,7},{7,4},{8,9},{9,10},{10,1... | collective-permute-start | bytes 1572872 | tf_op jit(solution)/shard_map/ppermute | solution.py:19
  82.0 4.0 copy-start.2
  82.0 4.0 copy-start.6
  88.0 30.0 %copy-start.7 = (bf16[256,64]{0,1:T(8,128)(2,1)S(1)}, bf16[256,64]{0,1:T(8,128)(2,1)}, u32[]{:S(2)}) copy-start(bf16[256,64]{0,1:T(8,128)(2,1)} %param.11) | copy-start | bytes 98308
  88.0 132.8 %reduce-scatter.4.cloned.1.call-start = ((), (), s32[]{:S(2)}) async-start(), calls=%async_computation.4 | async-start | bytes 10485760
  92.0 28.1 %copy-start.11 = (bf16[64,4096]{1,0:T(8,128)(2,1)S(1)}, bf16[64,4096]{1,0:T(8,128)(2,1)}, u32[]{:S(2)}) copy-start(bf16[64,4096]{1,0:T(8,128)(2,1)} %param.17) | copy-start | bytes 1572868
  235.0 107.5 %all-to-all-start.1 = ((f32[64,64,2,128]{3,0,2,1:T(8,128)}), f32[64,64,2,128]{3,0,2,1:T(8,128)}, u32[]{:S(2)}, u32[]{:S(2)}) async-start(f32[64,64,2,128]{3,0,2,1:T(8,128)} %fusion.12), calls=%async_computation.1 | async-start | bytes 8388608 | tf_op jit(solution)/shard_map/all_to_all | solution.py:56
  245.8 9.7 %copy-start.3 = (bf16[32,2,128,128]{3,2,1,0:T(8,128)(2,1)S(1)}, bf16[32,2,128,128]{3,2,1,0:T(8,128)(2,1)}, u32[]{:S(2)}) copy-start(bf16[32,2,128,128]{3,2,1,0:T(8,128)(2,1)} %param.13) | copy-start | bytes 6291460
  245.8 194.6 %all-reduce.3.cloned.1.call-start = ((), (), s32[]{:S(2)}) async-start(), calls=%async_computation.5 | async-start | bytes 262144 | tf_op jit(solution)/shard_map/psum | solution.py:45
  255.6 87.0 %copy-start.10 = (s32[1,64,2]{1,2,0:T(2,128)S(1)}, s32[1,64,2]{1,2,0:T(2,128)}, u32[]{:S(2)}) copy-start(s32[1,64,2]{1,2,0:T(2,128)} %param.14) | copy-start | bytes 1540
  342.5 8.4 %copy-start.4 = (f32[64,4096]{0,1:T(8,128)S(1)}, f32[64,4096]{0,1:T(8,128)}, u32[]{:S(2)}) copy-start(f32[64,4096]{0,1:T(8,128)} %copy.62) | copy-start | bytes 3145732
  348.9 94.5 %copy-start.1 = (bf16[256,64]{0,1:T(8,128)(2,1)S(1)}, bf16[256,64]{0,1:T(8,128)(2,1)}, u32[]{:S(2)}) copy-start(bf16[256,64]{0,1:T(8,128)(2,1)} %param.10) | copy-start | bytes 98308
Sparse Core Ops, SparseCore 0:
  88.1 29.8 all-gather.1
  137.6 83.1 reduce-scatter.3
  252.4 187.9 all-reduce.2
